TPU v7x, 32 devices: a whole 2x2x4 slice. The times are simulated.
32 devices in a mesh: ab: 16 (over z, y, core), ij: 2 (over x).
Axes of the slice: x: 2, y: 2, z: 4, core: 2. Of those that a mesh axis runs over, the one named last changes fastest.
Arguments:
- amplitudes: float32 [128, 2048], P('ab', 'ij'), may hold values from -6 to 6
- integrals: float32 [16384, 2048], P('ab'), may hold values from -0.125 to 0.125
- occ_pairs: float32 [128], P(('ab', 'ij')), may hold values from -2 to -0.5
- vir_pairs: float32 [16384], P('ab'), may hold values from 1 to 4
Outputs:
- update: float32 [128, 16384], P(('ab', 'ij'))
All inputs are finite; a program needn't handle non-finite values.
Results may differ from a plain program's by a relative error of at most 0.00007.
Values sent between devices are 32-bit elements; how exact they have to be, the bound alone decides.
No kernel may reach another device: no remote copies, remote signals or barrier semaphores. Data moves between devices by JAX's collectives and lax.ppermute only.
A program may use at most 64 MiB of HBM per device.

v0:
```python
import jax
import jax.numpy as jnp
from jax import lax
from jax.sharding import PartitionSpec as P


def contract(block_amps, integrals):
    return lax.dot_general(
        block_amps,
        integrals,
        (((1,), (1,)), ((), ())),
        precision=lax.Precision.HIGHEST,
        preferred_element_type=jnp.float32,
    )


def shards(amplitudes, integrals, occ_pairs, vir_pairs):
    arrived = lax.all_to_all(amplitudes, "ij", split_axis=0, concat_axis=1, tiled=True)
    slice_amps = lax.all_gather(arrived, "ab", axis=0, tiled=True)
    row_energy = lax.all_gather(occ_pairs, "ab", axis=0, tiled=True)
    groups = lax.axis_size("ab")
    per_device = occ_pairs.shape[0]
    panel_cols = integrals.shape[1]
    grouped = slice_amps.reshape(groups, per_device, panel_cols)
    energy_grouped = row_energy.reshape(groups, per_device)
    block_amps = grouped.reshape(-1, panel_cols)
    residual = contract(block_amps, integrals)
    block_energy = energy_grouped.reshape(-1)
    residual = residual / (vir_pairs[None, :] - block_energy[:, None])
    moved = lax.all_to_all(residual, "ab", split_axis=0, concat_axis=1, tiled=True)
    return moved


def solution(mesh):
    return jax.shard_map(
        shards,
        mesh=mesh,
        in_specs=(P("ab", "ij"), P("ab", None), P(("ab", "ij")), P("ab")),
        out_specs=P(("ab", "ij"), None),
        check_vma=False,
    )
```

profile of v0, /device:TPU:0, one launch (start us, length us, event | category | flops | bytes accessed | tf_op | source)
XLA Modules:
  0.0 86.3 jit_solution(3729236758331604290)
XLA Ops:
  0.0 1.4 %all_to_all.28 = f32[2,4,1024]{2,1,0:T(4,128)} reshape(f32[8,1024]{1,0:T(8,128)} %param.4) | data formatting | bytes 65536 | tf_op jit(solution)/shard_map/all_to_all | solution.py:18
  1.4 4.2 %all-to-all-start = ((f32[2,4,1024]{2,1,0:T(4,128)}), f32[2,4,1024]{2,1,0:T(4,128)S(1)}, u32[]{:S(2)}, u32[]{:S(2)}) async-start(f32[2,4,1024]{2,1,0:T(4,128)} %all_to_all.28), calls=%async_computation | async-start | bytes 65536 | tf_op jit(solution)/shard_map/all_to_all | solution.py:18
  5.6 1.3 %dynamic-slice = u32[1]{0:T(128)} dynamic-slice(u32[32]{0:T(128)} %constant.4, u32[]{:T(128)S(6)} %add), dynamic_slice_sizes={1} | dynamic-slice | bytes 12
  7.6 0.9 dynamic-update-slice
  8.5 34.0 %all-reduce = f32[64]{0:T(128)S(1)} all-reduce(f32[64]{0:T(128)S(1)} %dynamic-update-slice), channel_id=1, replica_groups=mesh['ab'=16,'ij'=2] {'ab'}, use_global_device_ids=true, to_apply=%add | all-reduce | flops 64 | bytes 512
  42.5 0.0 all-to-all-done
  42.5 18.7 %all-gather = f32[16,4,2048]{2,1,0:T(4,128)S(1)} all-gather(f32[1,4,2048]{2,1,0:T(4,128)S(1)} %bitcast.10), channel_id=1, replica_groups=mesh['ab'=16,'ij'=2] {'ab'}, dimensions={0}, use_global_device_ids=true | all-gather | bytes 557056 | tf_op jit(solution)/shard_map/all_gather | solution.py:19
  61.2 0.2 reshape.12
  61.4 10.5 %convolution_divide_fusion = f32[64,1024]{1,0:T(8,128)S(1)} fusion(f32[64,2048]{1,0:T(8,128)S(1)} %reshape.12, f32[1024,2048]{1,0:T(8,128)} %param.5, f32[64]{0:T(128)S(1)} %all-reduce, f32[1024]{0:T(1024)} %param.7), kind=kOutput, calls=%fused_computation | convolution fusion | flops 1610743808 | bytes 9179392 | tf_op jit(solution)/shard_map/dot_general | solution.py:8
  71.9 0.1 all_to_all.32
  72.0 13.6 %all_to_all.38 = f32[16,4,1024]{2,1,0:T(4,128)S(1)} all-to-all(f32[16,4,1024]{2,1,0:T(4,128)S(1)} %all_to_all.32), channel_id=1, replica_groups=mesh['ab'=16,'ij'=2] {'ab'}, dimensions={0} | all-to-all | bytes 524288 | tf_op jit(solution)/shard_map/all_to_all | solution.py:30
  85.6 0.7 copy.11
  (1 shorter events, 0.0 us)
Async XLA Ops:
  1.4 41.1 %all-to-all-start = ((f32[2,4,1024]{2,1,0:T(4,128)}), f32[2,4,1024]{2,1,0:T(4,128)S(1)}, u32[]{:S(2)}, u32[]{:S(2)}) async-start(f32[2,4,1024]{2,1,0:T(4,128)} %all_to_all.28), calls=%async_computation | async-start | bytes 65536 | tf_op jit(solution)/shard_map/all_to_all | solution.py:18
where the time goes:
time: 86.6 us; the launch traced here: 86.3 us
  blocking collectives  66.3 us (77%)
  matrix products  10.5 us (12%)
  local copies, waits for them, and re-layouts  4.52 us (5%)
  starting transfers between devices  4.23 us (5%)
    unnamed x1, blocking collectives  34 us
    all_gather x1, blocking collectives, shards(): slice_amps = lax.all_gather(arrived, 'ab', axis=0, tiled=True)  18.7 us
    all_to_all x1, blocking collectives, shards(): lax.all_to_all(residual, 'ab', split_axis=0, concat_axis=1, tiled=True)  13.6 us
    dot_general x1, matrix products, contract(): lax.dot_general(block_amps, integrals, (((1,), (1,)), ((), ())), precisio...  10.5 us
    all_to_all x1, starting transfers between devices, shards(): lax.all_to_all(amplitudes, 'ij', split_axis=0, concat_axis=1, tiled=True)  4.23 us
    unnamed x5, local copies, waits for them, and re-layouts  3.06 us
  transfers between devices with their start and end apart: 1, of which 0 were waited for; matrix products, arithmetic and copies ran while one was open for 3% of the time, Pallas kernels for 0%

commit v1 on v0

--- a/solution.py
+++ b/solution.py
@@ -2,6 +2,16 @@
 import jax.numpy as jnp
 from jax import lax
 from jax.sharding import PartitionSpec as P
+
+
+def pass_along(x, mesh_axis, dim):
+    n_dev = lax.axis_size(mesh_axis)
+    held, blocks = (x, [x])
+    for _ in range(n_dev - 1):
+        held = lax.ppermute(held, mesh_axis, [(i, (i + 1) % n_dev) for i in range(n_dev)])
+        blocks.insert(0, held)
+    flat = jnp.concatenate(blocks, axis=dim)
+    return jnp.roll(flat, (lax.axis_index(mesh_axis) + 1) * x.shape[dim], axis=dim)
 
 
 def contract(block_amps, integrals):
@@ -16,7 +26,7 @@
 
 def shards(amplitudes, integrals, occ_pairs, vir_pairs):
     arrived = lax.all_to_all(amplitudes, "ij", split_axis=0, concat_axis=1, tiled=True)
-    slice_amps = lax.all_gather(arrived, "ab", axis=0, tiled=True)
+    slice_amps = pass_along(arrived, "ab", 0)
     row_energy = lax.all_gather(occ_pairs, "ab", axis=0, tiled=True)
     groups = lax.axis_size("ab")
     per_device = occ_pairs.shape[0]

time: 86.6 us -> 155 us (1.79)
  waiting for transfers between devices: 0.01 us -> 84.5 us
  blocking collectives: 66.3 us -> 54.5 us
  starting transfers between devices: 4.23 us -> 0.04 us
    ppermute x0 -> x15, waiting for transfers between devices: none -> 84.5 us  [pass_along(): lax.ppermute(held, mesh_axis, [(i, (i + 1) % n_dev) for i in range(n_dev)])]
    all_gather x1 -> x0, blocking collectives: 18.7 us -> none  [shards(): slice_amps = lax.all_gather(arrived, 'ab', axis=0, tiled=True)]
    all_to_all x0 -> x1, blocking collectives: none -> 7.98 us  [shards(): lax.all_to_all(amplitudes, 'ij', split_axis=0, concat_axis=1, tiled=True)]
    all_to_all x1 -> x0, starting transfers between devices: 4.23 us -> none  [shards(): lax.all_to_all(amplitudes, 'ij', split_axis=0, concat_axis=1, tiled=True)]
  transfers between devices with their start and end apart: 1 -> 15, of which waited for: 0 -> 14; matrix products, arithmetic and copies ran while one was open for 3% -> 1% of each run, Pallas kernels for 0% -> 0%
where the time goes in v1:
time: 155 us; the launch traced here: 154 us
  waiting for transfers between devices  84.5 us (55%)
  blocking collectives  54.5 us (35%)
  matrix products  10.5 us (7%)
  local copies, waits for them, and re-layouts  4.24 us (3%)
    ppermute x15, waiting for transfers between devices, pass_along(): lax.ppermute(held, mesh_axis, [(i, (i + 1) % n_dev) for i in range(n_dev)])  84.5 us
    unnamed x1, blocking collectives  33.9 us
    all_to_all x1, blocking collectives, shards(): lax.all_to_all(residual, 'ab', split_axis=0, concat_axis=1, tiled=True)  12.6 us
    dot_general x1, matrix products, contract(): lax.dot_general(block_amps, integrals, (((1,), (1,)), ((), ())), precisio...  10.5 us
    all_to_all x1, blocking collectives, shards(): lax.all_to_all(amplitudes, 'ij', split_axis=0, concat_axis=1, tiled=True)  7.98 us
  transfers between devices with their start and end apart: 15, of which 14 were waited for; matrix products, arithmetic and copies ran while one was open for 1% of the time, Pallas kernels for 0%

profile of v1, /device:TPU:0, one launch (start us, length us, event | category | flops | bytes accessed | tf_op | source)
XLA Modules:
  0.0 154.5 jit_solution(9190398517280148582)
XLA Ops:
  0.0 0.8 all_to_all.28
  0.8 8.0 %all_to_all.38 = f32[2,4,1024]{2,1,0:T(4,128)S(1)} all-to-all(f32[2,4,1024]{2,1,0:T(4,128)S(1)} %all_to_all.28), channel_id=1, replica_groups=mesh['ab'=16,'ij'=2] {'ij'}, dimensions={0} | all-to-all | bytes 65536 | tf_op jit(solution)/shard_map/all_to_all | solution.py:28
  8.8 0.0 collective-permute-start
  8.8 6.0 %collective-permute-done = f32[4,2048]{1,0:T(4,128)S(1)} collective-permute-done((f32[4,2048]{1,0:T(4,128)S(1)}, f32[4,2048]{1,0:T(4,128)S(1)}, u32[]{:S(2)}, u32[]{:S(2)}) %collective-permute-start) | collective-permute-done | bytes 32800 | tf_op jit(solution)/shard_map/ppermute | solution.py:11
  14.8 0.0 collective-permute-start.1
  14.8 6.0 %collective-permute-done.1 = f32[4,2048]{1,0:T(4,128)S(1)} collective-permute-done((f32[4,2048]{1,0:T(4,128)S(1)}, f32[4,2048]{1,0:T(4,128)S(1)}, u32[]{:S(2)}, u32[]{:S(2)}) %collective-permute-start.1) | collective-permute-done | bytes 32800 | tf_op jit(solution)/shard_map/ppermute | solution.py:11
  20.8 0.0 collective-permute-start.2
  20.8 6.0 %collective-permute-done.2 = f32[4,2048]{1,0:T(4,128)S(1)} collective-permute-done((f32[4,2048]{1,0:T(4,128)S(1)}, f32[4,2048]{1,0:T(4,128)S(1)}, u32[]{:S(2)}, u32[]{:S(2)}) %collective-permute-start.2) | collective-permute-done | bytes 32800 | tf_op jit(solution)/shard_map/ppermute | solution.py:11
  26.9 0.0 collective-permute-start.3
  26.9 6.0 %collective-permute-done.3 = f32[4,2048]{1,0:T(4,128)S(1)} collective-permute-done((f32[4,2048]{1,0:T(4,128)S(1)}, f32[4,2048]{1,0:T(4,128)S(1)}, u32[]{:S(2)}, u32[]{:S(2)}) %collective-permute-start.3) | collective-permute-done | bytes 32800 | tf_op jit(solution)/shard_map/ppermute | solution.py:11
  32.9 0.0 collective-permute-start.4
  32.9 6.0 %collective-permute-done.4 = f32[4,2048]{1,0:T(4,128)S(1)} collective-permute-done((f32[4,2048]{1,0:T(4,128)S(1)}, f32[4,2048]{1,0:T(4,128)S(1)}, u32[]{:S(2)}, u32[]{:S(2)}) %collective-permute-start.4) | collective-permute-done | bytes 32800 | tf_op jit(solution)/shard_map/ppermute | solution.py:11
  38.9 0.0 collective-permute-start.5
  38.9 6.0 %collective-permute-done.5 = f32[4,2048]{1,0:T(4,128)S(1)} collective-permute-done((f32[4,2048]{1,0:T(4,128)S(1)}, f32[4,2048]{1,0:T(4,128)S(1)}, u32[]{:S(2)}, u32[]{:S(2)}) %collective-permute-start.5) | collective-permute-done | bytes 32800 | tf_op jit(solution)/shard_map/ppermute | solution.py:11
  45.0 0.0 collective-permute-start.6
  45.0 6.0 %collective-permute-done.6 = f32[4,2048]{1,0:T(4,128)S(1)} collective-permute-done((f32[4,2048]{1,0:T(4,128)S(1)}, f32[4,2048]{1,0:T(4,128)S(1)}, u32[]{:S(2)}, u32[]{:S(2)}) %collective-permute-start.6) | collective-permute-done | bytes 32800 | tf_op jit(solution)/shard_map/ppermute | solution.py:11
  51.0 0.0 collective-permute-start.7
  51.0 6.0 %collective-permute-done.7 = f32[4,2048]{1,0:T(4,128)S(1)} collective-permute-done((f32[4,2048]{1,0:T(4,128)S(1)}, f32[4,2048]{1,0:T(4,128)S(1)}, u32[]{:S(2)}, u32[]{:S(2)}) %collective-permute-start.7) | collective-permute-done | bytes 32800 | tf_op jit(solution)/shard_map/ppermute | solution.py:11
  57.1 0.0 collective-permute-start.8
  57.1 6.0 %collective-permute-done.8 = f32[4,2048]{1,0:T(4,128)S(1)} collective-permute-done((f32[4,2048]{1,0:T(4,128)S(1)}, f32[4,2048]{1,0:T(4,128)S(1)}, u32[]{:S(2)}, u32[]{:S(2)}) %collective-permute-start.8) | collective-permute-done | bytes 32800 | tf_op jit(solution)/shard_map/ppermute | solution.py:11
  63.1 0.0 collective-permute-start.9
  63.1 6.0 %collective-permute-done.9 = f32[4,2048]{1,0:T(4,128)S(1)} collective-permute-done((f32[4,2048]{1,0:T(4,128)S(1)}, f32[4,2048]{1,0:T(4,128)S(1)}, u32[]{:S(2)}, u32[]{:S(2)}) %collective-permute-start.9) | collective-permute-done | bytes 32800 | tf_op jit(solution)/shard_map/ppermute | solution.py:11
  69.1 0.0 collective-permute-start.10
  69.1 6.0 %collective-permute-done.10 = f32[4,2048]{1,0:T(4,128)S(1)} collective-permute-done((f32[4,2048]{1,0:T(4,128)S(1)}, f32[4,2048]{1,0:T(4,128)S(1)}, u32[]{:S(2)}, u32[]{:S(2)}) %collective-permute-start.10) | collective-permute-done | bytes 32800 | tf_op jit(solution)/shard_map/ppermute | solution.py:11
  75.2 0.0 collective-permute-start.11
  75.2 6.0 %collective-permute-done.11 = f32[4,2048]{1,0:T(4,128)S(1)} collective-permute-done((f32[4,2048]{1,0:T(4,128)S(1)}, f32[4,2048]{1,0:T(4,128)S(1)}, u32[]{:S(2)}, u32[]{:S(2)}) %collective-permute-start.11) | collective-permute-done | bytes 32800 | tf_op jit(solution)/shard_map/ppermute | solution.py:11
  81.2 0.0 collective-permute-start.12
  81.2 6.0 %collective-permute-done.12 = f32[4,2048]{1,0:T(4,128)S(1)} collective-permute-done((f32[4,2048]{1,0:T(4,128)S(1)}, f32[4,2048]{1,0:T(4,128)S(1)}, u32[]{:S(2)}, u32[]{:S(2)}) %collective-permute-start.12) | collective-permute-done | bytes 32800 | tf_op jit(solution)/shard_map/ppermute | solution.py:11
  87.2 0.0 collective-permute-start.13
  87.2 6.0 %collective-permute-done.13 = f32[4,2048]{1,0:T(4,128)S(1)} collective-permute-done((f32[4,2048]{1,0:T(4,128)S(1)}, f32[4,2048]{1,0:T(4,128)S(1)}, u32[]{:S(2)}, u32[]{:S(2)}) %collective-permute-start.13) | collective-permute-done | bytes 32800 | tf_op jit(solution)/shard_map/ppermute | solution.py:11
  93.3 0.0 collective-permute-start.14
  93.3 1.2 dynamic-slice
  95.2 0.9 dynamic-update-slice
  96.0 33.9 %all-reduce = f32[64]{0:T(128)S(1)} all-reduce(f32[64]{0:T(128)S(1)} %dynamic-update-slice), channel_id=1, replica_groups=mesh['ab'=16,'ij'=2] {'ab'}, use_global_device_ids=true, to_apply=%add | all-reduce | flops 64 | bytes 512
  129.9 0.0 collective-permute-done.14
  129.9 0.6 concatenate.6
  130.5 10.5 %convolution_divide_fusion = f32[64,1024]{1,0:T(8,128)S(1)} fusion(f32[1024,2048]{1,0:T(8,128)} %param.5, f32[128,2048]{1,0:T(8,128)S(1)} %concatenate.6, s32[]{:T(128)S(6)} %select_n.14, f32[64]{0:T(128)S(1)} %all-reduce, f32[1024]{0:T(1024)} %param.7), kind=kOutput, calls=%fused_computation | convolution fusion | flops 1610743808 | bytes 9179652 | tf_op jit(solution)/shard_map/dot_general | solution.py:18
  141.1 0.1 all_to_all.32
  141.1 12.6 %all_to_all.39 = f32[16,4,1024]{2,1,0:T(4,128)S(1)} all-to-all(f32[16,4,1024]{2,1,0:T(4,128)S(1)} %all_to_all.32), channel_id=1, replica_groups=mesh['ab'=16,'ij'=2] {'ab'}, dimensions={0} | all-to-all | bytes 524288 | tf_op jit(solution)/shard_map/all_to_all | solution.py:40
  153.7 0.7 copy.8
  (1 shorter events, 0.0 us)
Async XLA Ops:
  8.8 6.0 %collective-permute-start = (f32[4,2048]{1,0:T(4,128)S(1)}, f32[4,2048]{1,0:T(4,128)S(1)}, u32[]{:S(2)}, u32[]{:S(2)}) collective-permute-start(f32[4,2048]{1,0:T(4,128)S(1)} %bitcast.9), channel_id=1, source_target_pairs={{0,2},{2,4},{4,6},{6,8},{8,10},{10,12},{12,14},{14,16},{16,18},{18... | collective-permute-start | bytes 98312 | tf_op jit(solution)/shard_map/ppermute | solution.py:11
  14.8 6.0 %collective-permute-start.1 = (f32[4,2048]{1,0:T(4,128)S(1)}, f32[4,2048]{1,0:T(4,128)S(1)}, u32[]{:S(2)}, u32[]{:S(2)}) collective-permute-start(f32[4,2048]{1,0:T(4,128)S(1)} %collective-permute-done), channel_id=1, source_target_pairs={{0,2},{2,4},{4,6},{6,8},{8,10},{10,12},{12,14},{14,16},{16,18},{18... | collective-permute-start | bytes 98312 | tf_op jit(solution)/shard_map/ppermute | solution.py:11
  20.8 6.0 %collective-permute-start.2 = (f32[4,2048]{1,0:T(4,128)S(1)}, f32[4,2048]{1,0:T(4,128)S(1)}, u32[]{:S(2)}, u32[]{:S(2)}) collective-permute-start(f32[4,2048]{1,0:T(4,128)S(1)} %collective-permute-done.1), channel_id=1, source_target_pairs={{0,2},{2,4},{4,6},{6,8},{8,10},{10,12},{12,14},{14,16},{16,18},{18... | collective-permute-start | bytes 98312 | tf_op jit(solution)/shard_map/ppermute | solution.py:11
  26.9 6.0 %collective-permute-start.3 = (f32[4,2048]{1,0:T(4,128)S(1)}, f32[4,2048]{1,0:T(4,128)S(1)}, u32[]{:S(2)}, u32[]{:S(2)}) collective-permute-start(f32[4,2048]{1,0:T(4,128)S(1)} %collective-permute-done.2), channel_id=1, source_target_pairs={{0,2},{2,4},{4,6},{6,8},{8,10},{10,12},{12,14},{14,16},{16,18},{18... | collective-permute-start | bytes 98312 | tf_op jit(solution)/shard_map/ppermute | solution.py:11
  32.9 6.0 %collective-permute-start.4 = (f32[4,2048]{1,0:T(4,128)S(1)}, f32[4,2048]{1,0:T(4,128)S(1)}, u32[]{:S(2)}, u32[]{:S(2)}) collective-permute-start(f32[4,2048]{1,0:T(4,128)S(1)} %collective-permute-done.3), channel_id=1, source_target_pairs={{0,2},{2,4},{4,6},{6,8},{8,10},{10,12},{12,14},{14,16},{16,18},{18... | collective-permute-start | bytes 98312 | tf_op jit(solution)/shard_map/ppermute | solution.py:11
  38.9 6.0 %collective-permute-start.5 = (f32[4,2048]{1,0:T(4,128)S(1)}, f32[4,2048]{1,0:T(4,128)S(1)}, u32[]{:S(2)}, u32[]{:S(2)}) collective-permute-start(f32[4,2048]{1,0:T(4,128)S(1)} %collective-permute-done.4), channel_id=1, source_target_pairs={{0,2},{2,4},{4,6},{6,8},{8,10},{10,12},{12,14},{14,16},{16,18},{18... | collective-permute-start | bytes 98312 | tf_op jit(solution)/shard_map/ppermute | solution.py:11
  45.0 6.0 %collective-permute-start.6 = (f32[4,2048]{1,0:T(4,128)S(1)}, f32[4,2048]{1,0:T(4,128)S(1)}, u32[]{:S(2)}, u32[]{:S(2)}) collective-permute-start(f32[4,2048]{1,0:T(4,128)S(1)} %collective-permute-done.5), channel_id=1, source_target_pairs={{0,2},{2,4},{4,6},{6,8},{8,10},{10,12},{12,14},{14,16},{16,18},{18... | collective-permute-start | bytes 98312 | tf_op jit(solution)/shard_map/ppermute | solution.py:11
  51.0 6.0 %collective-permute-start.7 = (f32[4,2048]{1,0:T(4,128)S(1)}, f32[4,2048]{1,0:T(4,128)S(1)}, u32[]{:S(2)}, u32[]{:S(2)}) collective-permute-start(f32[4,2048]{1,0:T(4,128)S(1)} %collective-permute-done.6), channel_id=1, source_target_pairs={{0,2},{2,4},{4,6},{6,8},{8,10},{10,12},{12,14},{14,16},{16,18},{18... | collective-permute-start | bytes 98312 | tf_op jit(solution)/shard_map/ppermute | solution.py:11
  57.1 6.0 %collective-permute-start.8 = (f32[4,2048]{1,0:T(4,128)S(1)}, f32[4,2048]{1,0:T(4,128)S(1)}, u32[]{:S(2)}, u32[]{:S(2)}) collective-permute-start(f32[4,2048]{1,0:T(4,128)S(1)} %collective-permute-done.7), channel_id=1, source_target_pairs={{0,2},{2,4},{4,6},{6,8},{8,10},{10,12},{12,14},{14,16},{16,18},{18... | collective-permute-start | bytes 98312 | tf_op jit(solution)/shard_map/ppermute | solution.py:11
  63.1 6.0 %collective-permute-start.9 = (f32[4,2048]{1,0:T(4,128)S(1)}, f32[4,2048]{1,0:T(4,128)S(1)}, u32[]{:S(2)}, u32[]{:S(2)}) collective-permute-start(f32[4,2048]{1,0:T(4,128)S(1)} %collective-permute-done.8), channel_id=1, source_target_pairs={{0,2},{2,4},{4,6},{6,8},{8,10},{10,12},{12,14},{14,16},{16,18},{18... | collective-permute-start | bytes 98312 | tf_op jit(solution)/shard_map/ppermute | solution.py:11
  69.1 6.0 %collective-permute-start.10 = (f32[4,2048]{1,0:T(4,128)S(1)}, f32[4,2048]{1,0:T(4,128)S(1)}, u32[]{:S(2)}, u32[]{:S(2)}) collective-permute-start(f32[4,2048]{1,0:T(4,128)S(1)} %collective-permute-done.9), channel_id=1, source_target_pairs={{0,2},{2,4},{4,6},{6,8},{8,10},{10,12},{12,14},{14,16},{16,18},{18... | collective-permute-start | bytes 98312 | tf_op jit(solution)/shard_map/ppermute | solution.py:11
  75.2 6.0 %collective-permute-start.11 = (f32[4,2048]{1,0:T(4,128)S(1)}, f32[4,2048]{1,0:T(4,128)S(1)}, u32[]{:S(2)}, u32[]{:S(2)}) collective-permute-start(f32[4,2048]{1,0:T(4,128)S(1)} %collective-permute-done.10), channel_id=1, source_target_pairs={{0,2},{2,4},{4,6},{6,8},{8,10},{10,12},{12,14},{14,16},{16,18},{18... | collective-permute-start | bytes 98312 | tf_op jit(solution)/shard_map/ppermute | solution.py:11
  81.2 6.0 %collective-permute-start.12 = (f32[4,2048]{1,0:T(4,128)S(1)}, f32[4,2048]{1,0:T(4,128)S(1)}, u32[]{:S(2)}, u32[]{:S(2)}) collective-permute-start(f32[4,2048]{1,0:T(4,128)S(1)} %collective-permute-done.11), channel_id=1, source_target_pairs={{0,2},{2,4},{4,6},{6,8},{8,10},{10,12},{12,14},{14,16},{16,18},{18... | collective-permute-start | bytes 98312 | tf_op jit(solution)/shard_map/ppermute | solution.py:11
  87.2 6.0 %collective-permute-start.13 = (f32[4,2048]{1,0:T(4,128)S(1)}, f32[4,2048]{1,0:T(4,128)S(1)}, u32[]{:S(2)}, u32[]{:S(2)}) collective-permute-start(f32[4,2048]{1,0:T(4,128)S(1)} %collective-permute-done.12), channel_id=1, source_target_pairs={{0,2},{2,4},{4,6},{6,8},{8,10},{10,12},{12,14},{14,16},{16,18},{18... | collective-permute-start | bytes 98312 | tf_op jit(solution)/shard_map/ppermute | solution.py:11
  93.3 36.7 %collective-permute-start.14 = (f32[4,2048]{1,0:T(4,128)S(1)}, f32[4,2048]{1,0:T(4,128)S(1)}, u32[]{:S(2)}, u32[]{:S(2)}) collective-permute-start(f32[4,2048]{1,0:T(4,128)S(1)} %collective-permute-done.13), channel_id=1, source_target_pairs={{0,2},{2,4},{4,6},{6,8},{8,10},{10,12},{12,14},{14,16},{16,18},{18... | collective-permute-start | bytes 98312 | tf_op jit(solution)/shard_map/ppermute | solution.py:11
